TPU v7x, 256 devices: a whole 4x4x8 slice. The times are simulated.
256 devices in a mesh: dp: 8 (over x, z_hi), tensor: 8 (over y, core), expert: 4 (over z_lo).
Axes of the slice: x: 4, y: 4, z: 8 (z_hi: 2, z_lo: 4; z = z_hi * 4 + z_lo), core: 2. Of those that a mesh axis runs over, the one named last changes fastest.
Arguments:
- moe_input: bfloat16 [8192, 2048], P(('dp', 'tensor'), 'expert'), may hold values from -6 to 6
- grad_output: bfloat16 [8192, 2048], P(('dp', 'tensor'), 'expert'), may hold values from -6 to 6
- routes: int32 [8192, 8], P(('dp', 'tensor')), may hold values from 0 to 127, all different within a row; in each aligned block of 128 rows (0 to 127, 128 to 255, ...) at most 12 rows name the same one
- route_weight: float32 [8192, 8], P(('dp', 'tensor')), may hold values from 0.05 to 0.35
- capacity: int32 [128], replicated, may hold values from 6 to 12, as said below
- w_gate: bfloat16 [256, 384, 2048], P(('dp', 'tensor', 'expert')), may hold values from -0.125 to 0.125
- w_up: bfloat16 [256, 384, 2048], P(('dp', 'tensor', 'expert')), may hold values from -0.125 to 0.125
- w_down: bfloat16 [256, 384, 2048], P(('dp', 'tensor', 'expert')), may hold values from -0.21875 to 0.21875
Outputs:
- moe_output: bfloat16 [8192, 2048], P(('dp', 'tensor'), 'expert')
- grad_input: bfloat16 [8192, 2048], P(('dp', 'tensor'), 'expert')
- grad_gate: bfloat16 [256, 384, 2048], P(('dp', 'tensor', 'expert'))
- grad_up: bfloat16 [256, 384, 2048], P(('dp', 'tensor', 'expert'))
- grad_down: bfloat16 [256, 384, 2048], P(('dp', 'tensor', 'expert'))
Inputs may be any that keep to these rules, and one draw needn't show every extreme that they name: `routes`: each row names 8 different experts; within each aligned block of 128 rows (the rows of one device) no expert is named more than 12 times. Some expert has a capacity of exactly 12.
All inputs are finite; a program needn't handle non-finite values.
Results may differ from a plain program's by a relative error of at most 0.0071.
Values may be sent and summed in bfloat16 or wider, within the bound.
A program may use at most 128 MiB of HBM per device.

v0:
```python
import jax
import jax.numpy as jnp
from jax import lax
from jax.sharding import PartitionSpec as P


def swapped(x, axis, apart):
    return lax.ppermute(x, axis, [(i, i ^ 1 << apart) for i in range(lax.axis_size(axis))])


def expert_work(slot_rows, slot_cots, gate_w, up_w, down_w):
    gate_pre = jnp.einsum("smd,hd->smh", slot_rows, gate_w, preferred_element_type=jnp.float32)
    up_pre = jnp.einsum("smd,hd->smh", slot_rows, up_w, preferred_element_type=jnp.float32)
    sigmoid_gate = jax.nn.sigmoid(gate_pre)
    gate_act = gate_pre * sigmoid_gate
    hidden = (gate_act * up_pre).astype(jnp.bfloat16)
    out_part = jnp.einsum("smh,hd->smd", hidden, down_w, preferred_element_type=jnp.float32).astype(
        jnp.bfloat16
    )
    hidden_cot = jnp.einsum("smd,hd->smh", slot_cots, down_w, preferred_element_type=jnp.float32)
    gate_cot = (
        hidden_cot * up_pre * sigmoid_gate * (1.0 + gate_pre * (1.0 - sigmoid_gate))
    ).astype(jnp.bfloat16)
    up_cot = (hidden_cot * gate_act).astype(jnp.bfloat16)
    in_sum = jnp.einsum("smh,hd->smd", gate_cot, gate_w, preferred_element_type=jnp.float32)
    in_sum = in_sum + jnp.einsum("smh,hd->smd", up_cot, up_w, preferred_element_type=jnp.float32)
    in_part = in_sum.astype(jnp.bfloat16)
    grad_gate = jnp.einsum(
        "smh,smd->hd", gate_cot, slot_rows, preferred_element_type=jnp.float32
    ).astype(jnp.bfloat16)
    grad_up = jnp.einsum(
        "smh,smd->hd", up_cot, slot_rows, preferred_element_type=jnp.float32
    ).astype(jnp.bfloat16)
    grad_down = jnp.einsum(
        "smh,smd->hd", hidden, slot_cots, preferred_element_type=jnp.float32
    ).astype(jnp.bfloat16)
    return (out_part, in_part, grad_gate[None], grad_up[None], grad_down[None])


def fill_slots(inputs, cots, owners, weights):
    filled = owners >= 0
    source = jnp.maximum(owners, 0)
    slot_rows = jnp.where(filled[..., None], inputs[source], jnp.zeros((), inputs.dtype))
    slot_cots = jnp.where(
        filled[..., None], weights[..., None] * cots[source].astype(jnp.float32), 0.0
    )
    return (slot_rows, slot_cots.astype(jnp.bfloat16))


def shards(moe_input, grad_output, routes, route_weight, capacity, w_gate, w_up, w_down):
    groups = lax.axis_size(("dp", "tensor"))
    position = lax.axis_index("expert")
    parity = position // 2
    half_index = position % 2
    tok_rows = routes.shape[0]
    topk = routes.shape[1]
    experts = capacity.shape[0]
    slot_depth = 12 * tok_rows // experts
    slot_count = experts * slot_depth
    pair_count = tok_rows * topk
    col_quarter = moe_input.shape[1]
    full_width = col_quarter * lax.axis_size("expert")
    half_width = full_width // 2
    flat_routes = routes.reshape(pair_count)
    onehot = (flat_routes[:, None] == jnp.arange(experts, dtype=jnp.int32)[None, :]).astype(
        jnp.int32
    )
    before = jnp.cumsum(onehot, axis=0) - onehot
    pair_rank = jnp.sum(onehot * before, axis=1)
    pair_limit = jnp.sum(onehot * capacity[None, :], axis=1)
    pair_kept = pair_rank < pair_limit
    pair_place = jnp.where(pair_kept, flat_routes * slot_depth + pair_rank, slot_count)
    pair_token = jnp.arange(pair_count, dtype=jnp.int32) // topk
    flat_weight = route_weight.reshape(pair_count)
    slot_owner = jnp.full((slot_count,), -1, jnp.int32).at[pair_place].set(pair_token, mode="drop")
    slot_weight = jnp.zeros((slot_count,), jnp.float32).at[pair_place].set(flat_weight, mode="drop")
    whole_input, whole_cot = (
        lax.all_gather(moe_input, "expert", axis=1, tiled=True),
        lax.all_gather(grad_output, "expert", axis=1, tiled=True),
    )
    owners = lax.dynamic_index_in_dim(
        slot_owner.reshape(groups, 2, slot_depth), parity, 1, keepdims=False
    )
    weights = lax.dynamic_index_in_dim(
        slot_weight.reshape(groups, 2, slot_depth), parity, 1, keepdims=False
    )
    send_rows, send_cots = fill_slots(whole_input, whole_cot, owners, weights)
    got_rows, got_cots = (
        lax.all_to_all(send_rows, ("dp", "tensor"), split_axis=0, concat_axis=0, tiled=True),
        lax.all_to_all(send_cots, ("dp", "tensor"), split_axis=0, concat_axis=0, tiled=True),
    )
    out_part, in_part, grad_gate, grad_up, grad_down = expert_work(
        got_rows, got_cots, w_gate[0], w_up[0], w_down[0]
    )
    out_split = out_part.reshape(groups, slot_depth, 2, half_width)
    in_split = in_part.reshape(groups, slot_depth, 2, half_width)
    mine_out = lax.dynamic_index_in_dim(out_split, half_index, 2, keepdims=False)
    mine_in = lax.dynamic_index_in_dim(in_split, half_index, 2, keepdims=False)
    other_out = lax.dynamic_index_in_dim(out_split, 1 - half_index, 2, keepdims=False)
    other_in = lax.dynamic_index_in_dim(in_split, 1 - half_index, 2, keepdims=False)
    peer_out, peer_in = swapped((other_out, other_in), "expert", 0)
    expert_out = (mine_out.astype(jnp.float32) + peer_out.astype(jnp.float32)).astype(jnp.bfloat16)
    input_slot = (mine_in.astype(jnp.float32) + peer_in.astype(jnp.float32)).astype(jnp.bfloat16)
    back_out, back_in = (
        lax.all_to_all(expert_out, ("dp", "tensor"), split_axis=0, concat_axis=0, tiled=True),
        lax.all_to_all(input_slot, ("dp", "tensor"), split_axis=0, concat_axis=0, tiled=True),
    )
    flat_out = back_out.reshape(groups * slot_depth, half_width)
    flat_in = back_in.reshape(groups * slot_depth, half_width)
    matched = pair_kept & (flat_routes % 2 == parity)
    back_place = jnp.where(matched, flat_routes // 2 * slot_depth + pair_rank, 0)
    pair_scale = jnp.where(matched, flat_weight, 0.0)
    pair_mask = jnp.where(matched, 1.0, 0.0)
    partial_out = jnp.sum(
        (flat_out[back_place].astype(jnp.float32) * pair_scale[:, None]).reshape(
            tok_rows, topk, half_width
        ),
        axis=1,
    )
    partial_in = jnp.sum(
        (flat_in[back_place].astype(jnp.float32) * pair_mask[:, None]).reshape(
            tok_rows, topk, half_width
        ),
        axis=1,
    )
    which_half = (jnp.arange(2, dtype=jnp.int32) == half_index)[None, :, None]
    placed_out = jnp.where(which_half, partial_out[:, None, :], 0.0).reshape(tok_rows, full_width)
    placed_in = jnp.where(which_half, partial_in[:, None, :], 0.0).reshape(tok_rows, full_width)
    moe_output, grad_input = (
        lax.psum_scatter(placed_out, "expert", scatter_dimension=1, tiled=True),
        lax.psum_scatter(placed_in, "expert", scatter_dimension=1, tiled=True),
    )
    return (
        moe_output.astype(jnp.bfloat16),
        grad_input.astype(jnp.bfloat16),
        grad_gate,
        grad_up,
        grad_down,
    )


def solution(mesh):
    in_specs = (
        P(("dp", "tensor"), "expert"),
        P(("dp", "tensor"), "expert"),
        P(("dp", "tensor"), None),
        P(("dp", "tensor"), None),
        P(),
        P(("dp", "tensor", "expert"), None, None),
        P(("dp", "tensor", "expert"), None, None),
        P(("dp", "tensor", "expert"), None, None),
    )
    out_specs = (
        P(("dp", "tensor"), "expert"),
        P(("dp", "tensor"), "expert"),
        P(("dp", "tensor", "expert"), None, None),
        P(("dp", "tensor", "expert"), None, None),
        P(("dp", "tensor", "expert"), None, None),
    )
    return jax.shard_map(shards, mesh=mesh, in_specs=in_specs, out_specs=out_specs, check_vma=False)
```

profile of v0, /device:TPU:1, one launch (start us, length us, event | category | flops | bytes accessed | tf_op | source)
XLA Modules:
  0.0 627.3 jit_solution(496338516431408893)
XLA Ops:
  7.2 0.9 copy.60
  8.5 0.1 copy.62
  8.6 0.2 fusion.22
  8.8 0.1 copy.63
  9.0 1.2 select_reduce_fusion
  10.2 4.3 scatter_custom_fusion
  14.5 0.1 reshape.298
  14.7 0.1 maximum_reduce_fusion
  15.0 16.3 %all_gather.6 = bf16[128,2048]{1,0:T(8,128)(2,1)S(1)} all-gather(bf16[128,512]{1,0:T(8,128)(2,1)S(1)} %copy-done.8), channel_id=1, replica_groups=mesh['dp'=8,'tensor'=8,'expert'=4] {'expert'}, dimensions={1}, use_global_device_ids=true | all-gather | bytes 655360 | tf_op jit(solution)/shard_map/all_gather | solution.py:78
  31.3 4.2 gather_fusion
  35.6 6.1 reshape.310
  41.7 4.5 broadcast_select_fusion
  46.2 15.3 %all-to-all-start = ((bf16[64,12,2048]{2,1,0:T(8,128)(2,1)}), bf16[64,12,2048]{2,1,0:T(8,128)(2,1)}, u32[]{:S(2)}, u32[]{:S(2)}) async-start(bf16[64,12,2048]{2,1,0:T(8,128)(2,1)} %broadcast_select_fusion), calls=%async_computation | async-start | bytes 8388608 | tf_op jit(solution)/shard_map/all_to_all | solution.py:89
  61.5 0.1 copy.77
  61.7 4.3 scatter_custom_fusion.1
  66.0 0.1 reshape.302
  66.2 97.9 %all_gather.7 = bf16[128,2048]{1,0:T(8,128)(2,1)S(1)} all-gather(bf16[128,512]{1,0:T(8,128)(2,1)S(1)} %copy-done.9), channel_id=1, replica_groups=mesh['dp'=8,'tensor'=8,'expert'=4] {'expert'}, dimensions={1}, use_global_device_ids=true | all-gather | bytes 655360 | tf_op jit(solution)/shard_map/all_gather | solution.py:79
  164.1 4.3 gather_fusion.2
  168.4 6.4 %reshape.361 = f32[64,12,2048]{2,1,0:T(8,128)} reshape(bf16[768,2048]{1,0:T(8,128)(2,1)} %gather_fusion.2) | data formatting | bytes 9437184 | tf_op jit(solution)/shard_map/convert_element_type | solution.py:45
  174.8 5.2 select_convert_fusion
  180.1 13.6 %all-to-all-start.2 = ((bf16[64,12,2048]{2,1,0:T(8,128)(2,1)}), bf16[64,12,2048]{2,1,0:T(8,128)(2,1)}, u32[]{:S(2)}, u32[]{:S(2)}) async-start(bf16[64,12,2048]{2,1,0:T(8,128)(2,1)} %select_convert_fusion), calls=%async_computation.3 | async-start | bytes 8388608 | tf_op jit(solution)/shard_map/all_to_all | solution.py:90
  193.7 5.8 fusion.13
  199.6 5.2 fusion.17
  204.8 87.0 %all-to-all-done.2 = bf16[64,12,2048]{2,1,0:T(8,128)(2,1)} async-done(((bf16[64,12,2048]{2,1,0:T(8,128)(2,1)}), bf16[64,12,2048]{2,1,0:T(8,128)(2,1)}, u32[]{:S(2)}, u32[]{:S(2)}) %all-to-all-start.2) | async-done | bytes 3145760 | tf_op jit(solution)/shard_map/all_to_all | solution.py:90
  291.8 6.2 multiply_convert_fusion
  298.0 0.8 copy-done.12
  298.8 3.5 convolution_convert_fusion
  302.4 6.3 %reshape.299 = bf16[64,12,2,1024]{3,2,0,1:T(2,128)(2,1)} reshape(bf16[64,12,2048]{2,0,1:T(8,128)(2,1)} %convolution_convert_fusion) | data formatting | bytes 6291456 | tf_op jit(solution)/shard_map/reshape | solution.py:95
  308.7 1.8 fusion.15
  310.5 3.5 add_convert_fusion
  314.0 6.1 reshape.303
  320.2 27.6 %constant_dynamic-slice_fusion.1 = (bf16[64,12,1,1024]{3,2,0,1:T(2,128)(2,1)}, bf16[64,12,1,1024]{3,2,0,1:T(2,128)(2,1)}, bf16[64,12,1,1024]{3,2,0,1:T(2,128)(2,1)S(1)}, bf16[64,12,1,1024]{3,2,0,1:T(2,128)(2,1)S(1)}) fusion(bf16[64,12,2,1024]{3,2,0,1:T(2,128)(2,1)} %reshape.303, s32[]{:T(128)S(6)} %select_n.147, s32[]{:T(128)S(6)} %select_n.148, ...), kind=kLoop, calls=%fused_computation.96 | loop fusion | bytes 12582920 | tf_op jit(solution)/shard_map/jit(dynamic_index_in_dim)/dynamic_slice | solution.py:98
  347.7 0.6 copy.136
  348.4 33.5 %collective-permute-done = bf16[64,12,1024]{2,0,1:T(8,128)(2,1)S(1)} collective-permute-done((bf16[64,12,1024]{2,0,1:T(8,128)(2,1)S(1)}, bf16[64,12,1024]{2,0,1:T(8,128)(2,1)S(1)}, u32[]{:S(2)}, u32[]{:S(2)}) %collective-permute-start) | collective-permute-done | bytes 1572896 | tf_op jit(solution)/shard_map/ppermute | solution.py:8
  382.0 1.1 fusion.3
  383.1 2.2 copy.71
  385.3 8.7 %all-to-all-start.1 = ((bf16[64,12,1024]{2,1,0:T(8,128)(2,1)}), bf16[64,12,1024]{2,1,0:T(8,128)(2,1)}, u32[]{:S(2)}, u32[]{:S(2)}) async-start(bf16[64,12,1024]{2,1,0:T(8,128)(2,1)} %copy.71), calls=%async_computation.1 | async-start | bytes 4194304 | tf_op jit(solution)/shard_map/all_to_all | solution.py:105
  394.0 2.6 copy.135
  396.8 76.5 %collective-permute-done.1 = bf16[64,12,1024]{2,0,1:T(8,128)(2,1)S(1)} collective-permute-done((bf16[64,12,1024]{2,0,1:T(8,128)(2,1)S(1)}, bf16[64,12,1024]{2,0,1:T(8,128)(2,1)S(1)}, u32[]{:S(2)}, u32[]{:S(2)}) %collective-permute-start.1) | collective-permute-done | bytes 1572896 | tf_op jit(solution)/shard_map/ppermute | solution.py:8
  473.3 1.1 fusion.2
  474.4 2.2 copy.84
  476.6 13.5 %all-to-all-start.3 = ((bf16[64,12,1024]{2,1,0:T(8,128)(2,1)}), bf16[64,12,1024]{2,1,0:T(8,128)(2,1)}, u32[]{:S(2)}, u32[]{:S(2)}) async-start(bf16[64,12,1024]{2,1,0:T(8,128)(2,1)} %copy.84), calls=%async_computation.4 | async-start | bytes 4194304 | tf_op jit(solution)/shard_map/all_to_all | solution.py:106
  490.3 0.1 copy.76
  490.7 2.5 reshape.300
  493.2 5.4 gather_fusion.1
  498.5 2.9 fusion.1
  501.5 0.4 broadcast_in_dim.113
  501.8 0.3 copy.110
  502.2 32.8 %all-to-all-done.3 = bf16[64,12,1024]{2,1,0:T(8,128)(2,1)} async-done(((bf16[64,12,1024]{2,1,0:T(8,128)(2,1)}), bf16[64,12,1024]{2,1,0:T(8,128)(2,1)}, u32[]{:S(2)}, u32[]{:S(2)}) %all-to-all-start.3) | async-done | bytes 1572896 | tf_op jit(solution)/shard_map/all_to_all | solution.py:106
  535.0 2.5 reshape.304
  537.5 5.4 gather_fusion.3
  542.9 2.9 fusion
  545.8 0.4 broadcast_in_dim.119
  546.2 0.3 copy.111
  546.5 1.5 broadcast_select_fusion.1
  548.1 0.3 reduce-scatter.3.cloned.1.call-start
  548.3 0.5 reduce-scatter.3.cloned.1.call-update
  548.9 7.4 %fusion.6 = bf16[1,384,2048]{2,1,0:T(8,128)(2,1)} fusion(bf16[64,12,384]{2,0,1:T(8,128)(2,1)S(1)} %copy-done.13, bf16[64,12,2048]{2,1,0:T(8,128)(2,1)} %all-to-all-done.2), kind=kOutput, calls=%fused_computation.23 | convolution fusion | flops 1208745984 | bytes 5308416 | tf_op jit(solution)/shard_map/smh,smd->hd/dot_general | solution.py:34
  556.3 7.4 %fusion.5 = bf16[1,384,2048]{2,1,0:T(8,128)(2,1)} fusion(bf16[64,12,384]{2,0,1:T(8,128)(2,1)S(1)} %copy-done.7, bf16[64,12,2048]{2,1,0:T(8,128)(2,1)} %all-to-all-done), kind=kOutput, calls=%fused_computation.22 | convolution fusion | flops 1208745984 | bytes 5308416 | tf_op jit(solution)/shard_map/smh,smd->hd/dot_general | solution.py:31
  563.7 7.5 %fusion.4 = bf16[1,384,2048]{2,1,0:T(8,128)(2,1)} fusion(bf16[64,12,384]{2,0,1:T(8,128)(2,1)S(1)} %get-tuple-element.14, bf16[64,12,2048]{2,1,0:T(8,128)(2,1)} %all-to-all-done), kind=kOutput, calls=%fused_computation.21 | convolution fusion | flops 1208745984 | bytes 5308416 | tf_op jit(solution)/shard_map/smh,smd->hd/dot_general | solution.py:28
  571.2 13.1 %reduce-scatter.5.cloned.1.call-done = f32[128,512]{1,0:T(8,128)} async-done(((f32[128,2048]{1,0:T(8,128)}), f32[128,512]{1,0:T(8,128)}) %reduce-scatter.5.cloned.1.call-update) | async-done | bytes 262160 | tf_op jit(solution)/shard_map/reduce_scatter | solution.py:131
  584.4 1.6 convert_element_type.103
  586.0 32.5 %reduce-scatter.3.cloned.1.call-done = f32[128,512]{1,0:T(8,128)} async-done(((f32[128,2048]{1,0:T(8,128)}), f32[128,512]{1,0:T(8,128)}) %reduce-scatter.3.cloned.1.call-update) | async-done | bytes 262160 | tf_op jit(solution)/shard_map/reduce_scatter | solution.py:130
  618.5 1.6 convert_element_type.91
  (57 shorter events, 1.3 us)
Async XLA Ops:
  7.2 284.6 %copy-start = (bf16[1,384,2048]{2,1,0:T(8,128)(2,1)S(1)}, bf16[1,384,2048]{2,1,0:T(8,128)(2,1)}, u32[]{:S(2)}) copy-start(bf16[1,384,2048]{2,1,0:T(8,128)(2,1)} %param.15) | copy-start | bytes 4718596
  7.2 7.8 %copy-start.8 = (bf16[128,512]{1,0:T(8,128)(2,1)S(1)}, bf16[128,512]{1,0:T(8,128)(2,1)}, u32[]{:S(2)}) copy-start(bf16[128,512]{1,0:T(8,128)(2,1)} %param.8) | copy-start | bytes 393220
  46.2 15.3 %copy-start.11 = (f32[128,8]{0,1:T(8,128)S(1)}, f32[128,8]{0,1:T(8,128)}, u32[]{:S(2)}) copy-start(f32[128,8]{0,1:T(8,128)} %param.11) | copy-start | bytes 12292
  46.2 20.0 %copy-start.9 = (bf16[128,512]{1,0:T(8,128)(2,1)S(1)}, bf16[128,512]{1,0:T(8,128)(2,1)}, u32[]{:S(2)}) copy-start(bf16[128,512]{1,0:T(8,128)(2,1)} %param.9) | copy-start | bytes 393220
  46.2 133.9 %all-to-all-start = ((bf16[64,12,2048]{2,1,0:T(8,128)(2,1)}), bf16[64,12,2048]{2,1,0:T(8,128)(2,1)}, u32[]{:S(2)}, u32[]{:S(2)}) async-start(bf16[64,12,2048]{2,1,0:T(8,128)(2,1)} %broadcast_select_fusion), calls=%async_computation | async-start | bytes 8388608 | tf_op jit(solution)/shard_map/all_to_all | solution.py:89
  180.1 111.7 %all-to-all-start.2 = ((bf16[64,12,2048]{2,1,0:T(8,128)(2,1)}), bf16[64,12,2048]{2,1,0:T(8,128)(2,1)}, u32[]{:S(2)}, u32[]{:S(2)}) async-start(bf16[64,12,2048]{2,1,0:T(8,128)(2,1)} %select_convert_fusion), calls=%async_computation.3 | async-start | bytes 8388608 | tf_op jit(solution)/shard_map/all_to_all | solution.py:90
  193.7 5.9 copy-start.3
  298.0 0.8 copy-start.12
  302.4 6.3 %copy-start.4 = (bf16[1,384,2048]{2,1,0:T(8,128)(2,1)S(1)}, bf16[1,384,2048]{2,1,0:T(8,128)(2,1)}, u32[]{:S(2)}) copy-start(bf16[1,384,2048]{2,1,0:T(8,128)(2,1)} %param.13) | copy-start | bytes 4718596
  308.7 1.8 copy-start.5
  308.7 1.8 copy-start.6
  348.3 33.6 %collective-permute-start = (bf16[64,12,1024]{2,0,1:T(8,128)(2,1)S(1)}, bf16[64,12,1024]{2,0,1:T(8,128)(2,1)S(1)}, u32[]{:S(2)}, u32[]{:S(2)}) collective-permute-start(bf16[64,12,1024]{2,0,1:T(8,128)(2,1)S(1)} %bitcast.99), channel_id=1, source_target_pairs={{0,1},{1,0},{2,3},{3,2},{4,5},{5,4},{6,7},{7,6},{8,9},{9,8},{10,11... | collective-permute-start | bytes 4718600 | tf_op jit(solution)/shard_map/ppermute | solution.py:8
  385.3 91.3 %all-to-all-start.1 = ((bf16[64,12,1024]{2,1,0:T(8,128)(2,1)}), bf16[64,12,1024]{2,1,0:T(8,128)(2,1)}, u32[]{:S(2)}, u32[]{:S(2)}) async-start(bf16[64,12,1024]{2,1,0:T(8,128)(2,1)} %copy.71), calls=%async_computation.1 | async-start | bytes 4194304 | tf_op jit(solution)/shard_map/all_to_all | solution.py:105
  394.0 79.3 %copy-start.2 = (bf16[64,12,1,1024]{3,2,0,1:T(2,128)(2,1)S(1)}, bf16[64,12,1,1024]{3,2,0,1:T(2,128)(2,1)}, u32[]{:S(2)}) copy-start(bf16[64,12,1,1024]{3,2,0,1:T(2,128)(2,1)} %get-tuple-element.9) | copy-start | bytes 4718596
  396.7 76.6 %collective-permute-start.1 = (bf16[64,12,1024]{2,0,1:T(8,128)(2,1)S(1)}, bf16[64,12,1024]{2,0,1:T(8,128)(2,1)S(1)}, u32[]{:S(2)}, u32[]{:S(2)}) collective-permute-start(bf16[64,12,1024]{2,0,1:T(8,128)(2,1)S(1)} %bitcast.100), channel_id=1, source_target_pairs={{0,1},{1,0},{2,3},{3,2},{4,5},{5,4},{6,7},{7,6},{8,9},{9,8},{10,11... | collective-permute-start | bytes 4718600 | tf_op jit(solution)/shard_map/ppermute | solution.py:8
  474.4 16.0 %copy-start.10 = (s32[128,8]{0,1:T(8,128)S(1)}, s32[128,8]{0,1:T(8,128)}, u32[]{:S(2)}) copy-start(s32[128,8]{0,1:T(8,128)} %param.10) | copy-start | bytes 12292
  476.6 58.4 %all-to-all-start.3 = ((bf16[64,12,1024]{2,1,0:T(8,128)(2,1)}), bf16[64,12,1024]{2,1,0:T(8,128)(2,1)}, u32[]{:S(2)}, u32[]{:S(2)}) async-start(bf16[64,12,1024]{2,1,0:T(8,128)(2,1)} %copy.84), calls=%async_computation.4 | async-start | bytes 4194304 | tf_op jit(solution)/shard_map/all_to_all | solution.py:106
  490.2 94.2 %reduce-scatter.5.cloned.1.call-start = ((), (), s32[]{:S(2)}) async-start(), calls=%async_computation.7 | async-start | bytes 1310720 | tf_op jit(solution)/shard_map/reduce_scatter | solution.py:131
  546.5 2.3 copy-start.13
  548.1 70.4 %reduce-scatter.3.cloned.1.call-start = ((), (), s32[]{:S(2)}) async-start(), calls=%async_computation.6 | async-start | bytes 1310720 | tf_op jit(solution)/shard_map/reduce_scatter | solution.py:130
  548.9 7.5 %copy-start.7 = (bf16[64,12,384]{2,0,1:T(8,128)(2,1)S(1)}, bf16[64,12,384]{2,0,1:T(8,128)(2,1)}, u32[]{:S(2)}) copy-start(bf16[64,12,384]{2,0,1:T(8,128)(2,1)} %get-tuple-element.13) | copy-start | bytes 1769476
  563.7 56.4 %copy-start.1 = (bf16[1,384,2048]{2,1,0:T(8,128)(2,1)S(1)}, bf16[1,384,2048]{2,1,0:T(8,128)(2,1)}, u32[]{:S(2)}) copy-start(bf16[1,384,2048]{2,1,0:T(8,128)(2,1)} %param.15) | copy-start | bytes 4718596
Sparse Core Ops, SparseCore 0:
  548.2 36.1 reduce-scatter.4
  587.1 31.3 reduce-scatter.2
where the time goes:
time: 635 us; the launch traced here: 627 us
  waiting for transfers between devices  276 us (43%)
  blocking collectives  114 us (18%)
  local copies, waits for them, and re-layouts  97.8 us (15%)
  starting transfers between devices  51.7 us (8%)
  matrix products  48.5 us (8%)
  other arithmetic  24.3 us (4%)
  between operations  14.9 us (2%)
    ppermute x2, waiting for transfers between devices, swapped(): lax.ppermute(x, axis, [(i, i ^ 1 << apart) for i in range(lax.axis_size(a...  110 us
    all_gather x1, blocking collectives, shards(): lax.all_gather(grad_output, 'expert', axis=1, tiled=True)  97.9 us
    all_to_all x1, waiting for transfers between devices, shards(): lax.all_to_all(send_cots, ('dp', 'tensor'), split_axis=0, concat_axis=0,...  87 us
    all_to_all x1, waiting for transfers between devices, shards(): lax.all_to_all(input_slot, ('dp', 'tensor'), split_axis=0, concat_axis=0,...  32.8 us
    reduce_scatter x1, waiting for transfers between devices, shards(): lax.psum_scatter(placed_out, 'expert', scatter_dimension=1, tiled=True)  32.5 us
    dynamic_slice x1, local copies, waits for them, and re-layouts, shards(): mine_in = lax.dynamic_index_in_dim(in_split, half_index, 2, keepdims=False)  27.6 us
    all_gather x1, blocking collectives, shards(): lax.all_gather(moe_input, 'expert', axis=1, tiled=True)  16.3 us
    all_to_all x1, starting transfers between devices, shards(): lax.all_to_all(send_rows, ('dp', 'tensor'), split_axis=0, concat_axis=0,...  15.3 us
  transfers between devices with their start and end apart: 8, of which 6 were waited for; matrix products, arithmetic and copies ran while one was open for 12% of the time, Pallas kernels for 0%

commit v1 on v0

v1 whole, which is shorter than its diff:
```python
import functools
import jax
import jax.numpy as jnp
from jax import lax
from jax.experimental import pallas as pl
from jax.experimental.pallas import tpu as pltpu
from jax.sharding import PartitionSpec as P

MESH = pl.DeviceIdType.MESH
F32 = jnp.float32
BF16 = jnp.bfloat16
PLANE = ((1, 0), (0, 1), (3, 0), (0, 3), (1, 1), (3, 3), (1, 3), (3, 1), (2, 0), (0, 2), (2, 1), (1, 2), (2, 3), (3, 2), (2, 2))
PLANE_X = sum(o[0] * 4**i for i, o in enumerate(PLANE))
PLANE_Y = sum(o[1] * 4**i for i, o in enumerate(PLANE))
OTHERS = tuple((dx, dy, 0, 0) for dx, dy in PLANE) + (
    (0, 0, 1, 0), (0, 0, 7, 0), (0, 0, 0, 1), (0, 0, 4, 0), (0, 0, 4, 1))


def device(x, y, z, c):
    return ((x % 4) * 2 + (z % 8) // 4, (y % 4) * 2 + c % 2, z % 4)


def nn(a, b):
    return jnp.dot(a, b, preferred_element_type=F32)


def nt(a, b):
    return lax.dot_general(a, b, (((1,), (1,)), ((), ())), preferred_element_type=F32)


def tiles(count, body):
    def step(i, carry):
        body(i)
        return carry

    lax.fori_loop(0, count, step, 0)


def rows_of(i, size):
    return pl.ds(pl.multiple_of(i * size, size), size)


def kernel(tok_ref, cot_ref, meta_ref, ids_ref, wg, wu, wd,
           out_ref, gin_ref, gg, gu, gd,
           X, S, R, B, W, G, pre, hc, hid, cot2, cT, hT, Pm, Wf, PT, Wh, Wl, wsl, meta, FA, CS, CR, QS, QR,
           w_sem, g_sem, m_ssem, m_rsem, a_ssem, a_rsem, ac_ssem, ac_rsem, d_ssem, d_rsem, o_ssem, o_rsem,
           c_ssem, c_rsem, q_ssem, q_rsem):
    dp, tn, ex = lax.axis_index("dp"), lax.axis_index("tensor"), lax.axis_index("expert")
    x, y, z, c = dp // 2, tn // 2, (dp % 2) * 4 + ex, tn % 2
    me = x * 4 + y
    late = []

    def remote(src, dst, ssem, rsem, to):
        return pltpu.make_async_remote_copy(
            src_ref=src, dst_ref=dst, send_sem=ssem, recv_sem=rsem, device_id=to, device_id_type=MESH)

    barrier = pltpu.get_barrier_semaphore()
    for dx, dy, dz, dc in OTHERS:
        pl.semaphore_signal(barrier, inc=1, device_id=device(x + dx, y + dy, z + dz, c + dc), device_id_type=MESH)

    loads = []
    for q in range(4):
        for j, w in enumerate((wg, wu, wd)):
            cp = pltpu.make_async_copy(w.at[0, :, pl.ds(q * 512, 512)], W.at[q, pl.ds(j * 384, 384)], w_sem.at[q, j])
            cp.start()
            loads.append(cp)

    zq, zh = z % 4, z // 4
    X[0, c, zq, zh] = tok_ref[...]
    X[1, c, zq, zh] = cot_ref[...]
    own = c * 2 + zh
    meta[own] = meta_ref[...]
    pl.semaphore_wait(barrier, len(OTHERS))

    notes = []
    for i, (dz, dc) in enumerate(((0, 1), (4, 0), (4, 1))):
        cp = remote(meta.at[own], meta.at[own], m_ssem.at[i], m_rsem.at[i], device(x, y, z + dz, c + dc))
        cp.start()
        notes.append(cp)

    def piece(arr, pz, half=None, core=None):
        pz = (pz + 8) % 8
        ref = X.at[arr, c if core is None else core, pz % 4, pz // 4]
        return ref if half is None else ref.at[pl.ds(half * 64, 64)]

    def ring_send(arr, s):
        for d, sgn in enumerate((1, -1)):
            src = piece(arr, z - sgn * s, d if s == 3 else None)
            cp = remote(src, src, a_ssem.at[arr, d, s], a_rsem.at[arr, d, s], device(x, y, z + sgn + 8, c))
            cp.start()
            late.append(cp)

    def ring_wait(arr, s):
        for d, sgn in enumerate((1, -1)):
            dst = piece(arr, z - sgn * (s + 1), d if s == 3 else None)
            remote(dst, dst, a_ssem.at[arr, d, s], a_rsem.at[arr, d, s], device(x, y, z + sgn + 8, c)).wait_recv()

    def core_send(arr, off):
        src = piece(arr, z + off)
        cp = remote(src, src, ac_ssem.at[arr, off + 3], ac_rsem.at[arr, off + 3], device(x, y, z, c + 1))
        cp.start()
        late.append(cp)

    def core_wait(arr, off):
        dst = piece(arr, z + off, core=1 - c)
        remote(dst, dst, ac_ssem.at[arr, off + 3], ac_rsem.at[arr, off + 3], device(x, y, z, c + 1)).wait_recv()

    def spread(src, dst, ssem, rsem, arr, q):
        mine = pl.ds(pl.multiple_of(me * 48, 48), 48)
        dst[arr, q, mine] = src[arr, q, mine]

        def one(i, carry):
            tx, ty = carry
            px, py = (x + tx % 4) % 4, (y + ty % 4) % 4
            there = pl.ds(pl.multiple_of((px * 4 + py) * 48, 48), 48)
            remote(src.at[arr, q, there], dst.at[arr, q, mine], ssem.at[arr, q], rsem.at[arr, q],
                   device(px, py, z, c)).start()
            return tx // 4, ty // 4

        lax.fori_loop(0, 15, one, (jnp.int32(PLANE_X), jnp.int32(PLANE_Y)))

    def all_of(ref, sem, arr, q):
        part = ref.at[arr, q, pl.ds(0, 720)]
        pltpu.make_async_copy(part, part, sem.at[arr, q]).wait()

    def select(arr, rel):
        q = (z + rel) % 4
        for off in {2: (2, -2), 1: (1, -3), 3: (-1, 3), 0: (0, 4)}[rel]:
            core_wait(arr, off)

        def body(i):
            m = rows_of(i, 256)
            v = nn(Pm[m, 0:256], X[arr, 0, q].reshape(256, 512)) + nn(Pm[m, 256:512], X[arr, 1, q].reshape(256, 512))
            if arr == 1:
                v = v * wsl[m, 0:1]
            S[arr, q, m] = v.astype(BF16)

        tiles(3, body)
        spread(S, R, d_ssem, d_rsem, arr, q)

    ring_send(0, 0)
    core_send(0, 0)
    for cp in notes:
        cp.wait()

    upper = (lax.broadcasted_iota(jnp.int32, (128, 128), 0) < lax.broadcasted_iota(jnp.int32, (128, 128), 1))
    upper = upper.astype(F32).astype(BF16)

    def build(i):
        m = rows_of(i, 256)
        rank = ids_ref[m, 4:5]
        total = jnp.zeros((256, 1), F32)
        for b in range(4):
            want = ids_ref[m, b:b + 1]
            hit = jnp.zeros((256, 128), F32)
            weight = jnp.zeros((256, 128), F32)
            for k in range(8):
                same = want == meta[b, k:k + 1, :]
                hit = jnp.where(same, 1.0, hit)
                weight = jnp.where(same, meta[b, k + 8:k + 9, :], weight)
            before = nn(hit.astype(BF16), upper)
            chosen = before == rank
            hit = jnp.where(chosen, hit, 0.0)
            weight = jnp.where(chosen, weight, 0.0)
            Pm[m, b * 128:(b + 1) * 128] = hit.astype(BF16)
            Wf[m, b * 128:(b + 1) * 128] = weight
            total = total + jnp.sum(weight, axis=1, keepdims=True)
        wsl[m] = jnp.broadcast_to(total, (256, 128))

    tiles(3, build)

    for arr in (0, 1):
        ring_wait(arr, 0)
        ring_send(arr, 1)
        core_send(arr, 1)
        core_send(arr, -1)
        ring_wait(arr, 1)
        ring_send(arr, 2)
        core_send(arr, 2)
        core_send(arr, -2)
        select(arr, 2)
        ring_wait(arr, 2)
        ring_send(arr, 3)
        core_send(arr, 3)
        core_send(arr, -3)
        if arr == 0:
            ring_send(1, 0)
            core_send(1, 0)
        select(arr, 1)
        select(arr, 3)
        ring_wait(arr, 3)
        core_send(arr, 4)
        select(arr, 0)

    for cp in loads:
        cp.wait()

    for k, rel in enumerate((2, 1, 3, 0)):
        q = (z + rel) % 4
        all_of(R, d_rsem, 0, q)

        def body(i, k=k, q=q):
            m = rows_of(i, 256)
            v = nt(R[0, q, m], W[q, 0:768])
            pre[m] = v if k == 0 else pre[m] + v

        tiles(3, body)

    def act(i):
        m = rows_of(i, 128)
        g, u = pre[m, 0:384], pre[m, 384:768]
        hid[m] = (g * jax.nn.sigmoid(g) * u).astype(BF16)

    tiles(6, act)

    for rel in (0, 1, 3, 2):
        q = (z + rel) % 4
        all_of(S, d_ssem, 0, q)

        def body(i, q=q):
            m = rows_of(i, 256)
            S[0, q, m] = nn(hid[m], W[q, 768:1152]).astype(BF16)

        tiles(3, body)
        spread(S, B, o_ssem, o_rsem, 0, q)

    def turn(i):
        m = rows_of(i, 256)
        for b in range(4):
            t = pl.ds(b * 128, 128)
            weight = Wf[m, b * 128:(b + 1) * 128].T
            high = weight.astype(BF16)
            Wh[t, m] = high
            Wl[t, m] = (weight - high.astype(F32)).astype(BF16)
            PT[t, m] = Pm[m, b * 128:(b + 1) * 128].astype(F32).T.astype(BF16)

    tiles(3, turn)

    for k, rel in enumerate((2, 1, 3, 0)):
        q = (z + rel) % 4
        all_of(R, d_rsem, 1, q)

        def body(i, k=k, q=q):
            m = rows_of(i, 256)
            v = nt(R[1, q, m], W[q, 768:1152])
            hc[m] = v if k == 0 else hc[m] + v

        tiles(3, body)

    def cots(i):
        m = rows_of(i, 128)
        g, u, h = pre[m, 0:384], pre[m, 384:768], hc[m]
        s = jax.nn.sigmoid(g)
        cot2[m, 0:384] = (h * u * s * (1.0 + g * (1.0 - s))).astype(BF16)
        cot2[m, 384:768] = (h * (g * s)).astype(BF16)

    tiles(6, cots)

    for rel in (0, 1, 3, 2):
        q = (z + rel) % 4
        all_of(S, d_ssem, 1, q)

        def body(i, q=q):
            m = rows_of(i, 256)
            S[1, q, m] = nn(cot2[m], W[q, 0:768]).astype(BF16)

        tiles(3, body)
        spread(S, B, o_ssem, o_rsem, 1, q)

    def turn2(i):
        m = rows_of(i, 128)
        cT[:, m] = cot2[m].astype(F32).T.astype(BF16)
        hT[:, m] = hid[m].astype(F32).T.astype(BF16)

    tiles(6, turn2)
    stores = []
    for q in range(4):
        def body(i, q=q):
            m = rows_of(i, 256)
            G[q, m] = nn(cT[m], R[0, q]).astype(BF16)

        tiles(3, body)
        G[q, 768:1152] = nn(hT[...], R[1, q]).astype(BF16)
        for j, o in enumerate((gg, gu, gd)):
            cp = pltpu.make_async_copy(G.at[q, pl.ds(j * 384, 384)], o.at[0, :, pl.ds(q * 512, 512)], g_sem.at[q, j])
            cp.start()
            stores.append(cp)

    def process(arr, rel):
        q = (z + rel) % 4
        all_of(B, o_rsem, arr, q)

        def summed(core):
            t = rows_of(core, 256)
            if arr == 0:
                return nn(Wh[t], B[0, q]) + nn(Wl[t], B[0, q])
            return nn(PT[t], B[1, q])

        CS[arr, q] = summed(1 - c).astype(BF16)
        cp = remote(CS.at[arr, q], CR.at[arr, q], c_ssem.at[arr, q], c_rsem.at[arr, q], device(x, y, z, c + 1))
        cp.start()
        late.append(cp)
        FA[arr, q] = summed(c)
        return cp

    def total(arr, d, low=0, size=128):
        d = (d + 8) % 8
        t = pl.ds(pl.multiple_of((d // 4) * 128 + low, 64), size)
        return FA[arr, d % 4, t] + CR[arr, d % 4, t].astype(F32)

    def back_send(arr, s):
        for d, sgn in enumerate((1, -1)):
            dest = z + sgn * (4 - s)
            if s == 0:
                QS[arr, d, 0, d * 64:d * 64 + 64] = total(arr, dest, d * 64, 64).astype(BF16)
                src, dst = QS.at[arr, d, 0, pl.ds(d * 64, 64)], QR.at[arr, d, 0, pl.ds(d * 64, 64)]
            else:
                back_wait(arr, d, s - 1)
                if s == 1:
                    h = slice(d * 64, d * 64 + 64)
                    o = (1 - d) * 64
                    QS[arr, d, 1, h] = (total(arr, dest, d * 64, 64) + QR[arr, d, 0, h].astype(F32)).astype(BF16)
                    QS[arr, d, 1, o:o + 64] = total(arr, dest, o, 64).astype(BF16)
                else:
                    QS[arr, d, s] = (total(arr, dest) + QR[arr, d, s - 1].astype(F32)).astype(BF16)
                src, dst = QS.at[arr, d, s], QR.at[arr, d, s]
            cp = remote(src, dst, q_ssem.at[arr, d, s], q_rsem.at[arr, d, s], device(x, y, z + sgn + 8, c))
            cp.start()
            late.append(cp)

    def back_wait(arr, d, s):
        dst = QR.at[arr, d, s, pl.ds(d * 64, 64)] if s == 0 else QR.at[arr, d, s]
        remote(dst, dst, q_ssem.at[arr, d, s], q_rsem.at[arr, d, s], device(x, y, z + 1, c)).wait_recv()

    for arr, o_ref in ((0, out_ref), (1, gin_ref)):
        process(arr, 0).wait_recv()
        back_send(arr, 0)
        first = process(arr, 1)
        process(arr, 3).wait_recv()
        first.wait_recv()
        back_send(arr, 1)
        process(arr, 2).wait_recv()
        back_send(arr, 2)
        back_send(arr, 3)
        back_wait(arr, 0, 3)
        back_wait(arr, 1, 3)
        o_ref[...] = (total(arr, z) + QR[arr, 0, 3].astype(F32) + QR[arr, 1, 3].astype(F32)).astype(BF16)

    for arr in (0, 1):
        for q in range(4):
            all_of(S, o_ssem, arr, q)
    for cp in late:
        cp.wait_send()
    for cp in stores:
        cp.wait()


def shards(moe_input, grad_output, routes, route_weight, capacity, w_gate, w_up, w_down):
    dp, tn, ex = lax.axis_index("dp"), lax.axis_index("tensor"), lax.axis_index("expert")
    meta = jnp.concatenate([routes.astype(F32).T, route_weight.T], axis=0)
    row = jnp.arange(768, dtype=jnp.int32)
    chip, block, rank = row // 48, row % 48 // 12, row % 12
    group = ((chip // 4) * 2 + dp % 2) * 8 + (chip % 4) * 2 + tn % 2
    expert = 2 * group + ex // 2
    open_slot = rank < capacity[expert]
    lane = jnp.arange(8, dtype=jnp.int32)[None, :]
    ids = jnp.where((lane == block[:, None]) & open_slot[:, None], expert[:, None], -1)
    ids = jnp.where(lane == 4, rank[:, None], ids).astype(F32)
    vmem = pl.BlockSpec(memory_space=pltpu.VMEM)
    hbm = pl.BlockSpec(memory_space=pl.ANY)
    dma = pltpu.SemaphoreType.DMA
    grad = jax.ShapeDtypeStruct((1, 384, 2048), BF16)
    tok = jax.ShapeDtypeStruct((128, 512), BF16)
    big = pltpu.VMEM((2, 4, 768, 512), BF16)
    return pl.pallas_call(
        kernel,
        out_shape=(tok, tok, grad, grad, grad),
        in_specs=[vmem] * 4 + [hbm] * 3,
        out_specs=(vmem, vmem, hbm, hbm, hbm),
        scratch_shapes=[
            pltpu.VMEM((2, 2, 4, 2, 128, 512), BF16),
            big, big, big,
            pltpu.VMEM((4, 1152, 512), BF16),
            pltpu.VMEM((4, 1152, 512), BF16),
            pltpu.VMEM((768, 768), F32),
            pltpu.VMEM((768, 384), F32),
            pltpu.VMEM((768, 384), BF16),
            pltpu.VMEM((768, 768), BF16),
            pltpu.VMEM((768, 768), BF16),
            pltpu.VMEM((384, 768), BF16),
            pltpu.VMEM((768, 512), BF16),
            pltpu.VMEM((768, 512), F32),
            pltpu.VMEM((512, 768), BF16),
            pltpu.VMEM((512, 768), BF16),
            pltpu.VMEM((512, 768), BF16),
            pltpu.VMEM((768, 128), F32),
            pltpu.VMEM((4, 16, 128), F32),
            pltpu.VMEM((2, 4, 256, 512), F32),
            pltpu.VMEM((2, 4, 256, 512), BF16),
            pltpu.VMEM((2, 4, 256, 512), BF16),
            pltpu.VMEM((2, 2, 4, 128, 512), BF16),
            pltpu.VMEM((2, 2, 4, 128, 512), BF16),
            dma((4, 3)), dma((4, 3)), dma((3,)), dma((3,)),
            dma((2, 2, 4)), dma((2, 2, 4)), dma((2, 8)), dma((2, 8)),
            dma((2, 4)), dma((2, 4)), dma((2, 4)), dma((2, 4)),
            dma((2, 4)), dma((2, 4)), dma((2, 2, 4)), dma((2, 2, 4)),
        ],
        compiler_params=pltpu.CompilerParams(
            collective_id=0, has_side_effects=True, vmem_limit_bytes=60 * 2**20),
        cost_estimate=pl.CostEstimate(flops=11 * 10**9, bytes_accessed=10**7, transcendentals=10**6),
        name="moe_step",
    )(moe_input, grad_output, meta, ids, w_gate, w_up, w_down)


def solution(mesh):
    tok = P(("dp", "tensor"), "expert")
    row = P(("dp", "tensor"), None)
    weight = P(("dp", "tensor", "expert"), None, None)
    return jax.shard_map(
        shards, mesh=mesh, in_specs=(tok, tok, row, row, P(), weight, weight, weight),
        out_specs=(tok, tok, weight, weight, weight), check_vma=False)
```

time: 635 us -> 200 us (0.31)
  waiting for transfers between devices: 276 us -> 0 us
  Pallas kernels: 0 us -> 180 us
  blocking collectives: 114 us -> 0 us
  local copies, waits for them, and re-layouts: 97.8 us -> 13.9 us
  starting transfers between devices: 51.7 us -> 0 us
  matrix products: 48.5 us -> 0 us
  other arithmetic: 24.3 us -> 3.55 us
  between operations: 14.9 us -> 0.72 us
    pallas_call x0 -> x1, Pallas kernels: none -> 180 us  [shards(): pl.pallas_call(kernel, out_shape=(tok, tok, grad, grad, grad), in_specs=[...]
    all_to_all x4 -> x0, waiting for transfers between devices: 120 us -> none  [the longest x1 87 us: shards(): lax.all_to_all(send_cots, ('dp', 'tensor'), split_axis=0, concat_axis=0,...]
    all_gather x2 -> x0, blocking collectives: 114 us -> none  [the longest x1 97.9 us: shards(): lax.all_gather(grad_output, 'expert', axis=1, tiled=True)]
    ppermute x2 -> x0, waiting for transfers between devices: 110 us -> none  [swapped(): lax.ppermute(x, axis, [(i, i ^ 1 << apart) for i in range(lax.axis_size(a...]
    all_to_all x4 -> x0, starting transfers between devices: 51.2 us -> none  [the longest x1 15.3 us: shards(): lax.all_to_all(send_rows, ('dp', 'tensor'), split_axis=0, concat_axis=0,...]
    dot_general x9 -> x0, matrix products: 48.5 us -> none  [the longest x1 7.52 us: expert_work(): jnp.einsum('smh,smd->hd', gate_cot, slot_rows, preferred_element_type=jnp...]
    reduce_scatter x2 -> x0, waiting for transfers between devices: 45.6 us -> none  [the longest x1 32.5 us: shards(): lax.psum_scatter(placed_out, 'expert', scatter_dimension=1, tiled=True)]
    dynamic_slice x2 -> x0, local copies, waits for them, and re-layouts: 27.6 us -> none  [the longest x1 27.6 us: shards(): mine_in = lax.dynamic_index_in_dim(in_split, half_index, 2, keepdims=False)]
  transfers between devices with their start and end apart: 8 -> 0, of which waited for: 6 -> 0; matrix products, arithmetic and copies ran while one was open for 12% -> 0% of each run, Pallas kernels for 0% -> 0%
where the time goes in v1:
time: 200 us; the launch traced here: 198 us
  Pallas kernels  180 us (90%)
  local copies, waits for them, and re-layouts  13.9 us (7%)
  other arithmetic  3.55 us (2%)
    pallas_call x1, Pallas kernels, shards(): pl.pallas_call(kernel, out_shape=(tok, tok, grad, grad, grad), in_specs=[...  180 us
    unnamed x11, local copies, waits for them, and re-layouts  9.11 us
    gather x1, local copies, waits for them, and re-layouts, shards(): open_slot = rank < capacity[expert]  4.79 us

profile of v1, /device:TPU:1, one launch (start us, length us, event | category | flops | bytes accessed | tf_op | source)
XLA Modules:
  0.0 198.5 jit_solution(3016131416440733205)
XLA Ops:
  0.6 0.0 copy-start
  0.7 0.7 convert_bitcast_fusion
  1.4 1.3 pad_maximum_fusion.meta_ref
  2.7 0.1 fusion.22
  2.8 0.0 copy-done
  2.8 4.8 %gather_fusion = s32[768]{0:T(1024)S(1)} fusion(s32[128]{0:T(128)S(1)} %copy-done, s32[1024]{0:T(1024)S(1)} %pad_clamp_fusion), kind=kCustom, calls=%fused_computation | custom fusion | bytes 9216 | tf_op jit(solution)/shard_map/gather | solution.py:365
  7.6 1.5 select_convert_fusion.ids_ref
  9.1 180.3 %moe_step.1 = (bf16[128,512]{1,0:T(8,128)(2,1)}, bf16[128,512]{1,0:T(8,128)(2,1)}, bf16[1,384,2048]{2,1,0:T(8,128)(2,1)}, bf16[1,384,2048]{2,1,0:T(8,128)(2,1)}, bf16[1,384,2048]{2,1,0:T(8,128)(2,1)}) custom-call(bf16[128,512]{1,0:T(8,128)(2,1)} %tok_ref.1, bf16[128,512]{1,0:T(8,128)(2,1)} %cot_ref.1, f32[16,128]{1,0:T(8,128)} %pad_maximum_fusion.meta_ref, ...), custom_call_target="tpu_custom_call" | custom-call | flops 11000000512 | bytes 10000000 | tf_op jit(solution)/shard_map/moe_step/pallas_call | solution.py:375
  189.4 1.6 copy.18
  190.9 1.6 copy.19
  192.5 0.0 copy-start.2
  192.5 2.8 %copy.20 = bf16[1,384,2048]{2,1,0:T(8,128)(2,1)} copy(bf16[1,384,2048]{2,1,0:T(8,128)(2,1)} %get-tuple-element.14) | data formatting | bytes 3145728
  195.4 0.0 copy-done.2
  195.4 0.0 copy-start.1
  195.4 1.1 copy.21
  196.5 0.8 copy-done.1
  197.3 1.1 copy.22
  (5 shorter events, 0.1 us)
Async XLA Ops:
  0.6 2.1 %copy-start = (s32[128]{0:T(128)S(1)}, s32[128]{0:T(128)}, u32[]{:S(2)}) copy-start(s32[128]{0:T(128)} %param.12) | copy-start | bytes 1540
  192.5 2.9 %copy-start.2 = (bf16[1,384,2048]{2,1,0:T(8,128)(2,1)S(1)}, bf16[1,384,2048]{2,1,0:T(8,128)(2,1)}, u32[]{:S(2)}) copy-start(bf16[1,384,2048]{2,1,0:T(8,128)(2,1)} %get-tuple-element.15) | copy-start | bytes 4718596
  195.4 2.0 copy-start.1
